TPU v7x, 512 devices: a whole 4x8x8 slice. The times are simulated.
512 devices in a mesh: ctx: 64 (over z_hi, y, core), tp: 8 (over x, z_lo).
Axes of the slice: x: 4, y: 8, z: 8 (z_hi: 4, z_lo: 2; z = z_hi * 2 + z_lo), core: 2. Of those that a mesh axis runs over, the one named last changes fastest.
Arguments:
- query_in: bfloat16 [1024, 16384], P('tp', 'ctx'), may hold values from -6 to 6
- key_in: bfloat16 [1024, 16384], P('tp', 'ctx'), may hold values from -6 to 6
- value_in: bfloat16 [1024, 16384], P('tp', 'ctx'), may hold values from -6 to 6
- short_kernel: float32 [3, 1024, 7], P(None, 'tp'), may hold values from -2 to 2
- basis_weight: float32 [64, 33], replicated, may hold values from -96 to 96
- basis_bias: float32 [64], replicated, may hold values from -3.140625 to 3.140625
- filter_proj: float32 [1024, 64], P('tp'), may hold values from -0.75 to 0.75
- decay_rate: float32 [1024], P('tp'), as said below
- skip_gain: float32 [1024], P('tp'), may hold values from -3 to 3
- grad_out: bfloat16 [1024, 16384], P('tp', 'ctx'), may hold values from -6 to 6
Outputs:
- mixed: bfloat16 [1024, 16384], P('tp', 'ctx')
- grad_query: bfloat16 [1024, 16384], P('tp', 'ctx')
- grad_key: bfloat16 [1024, 16384], P('tp', 'ctx')
- grad_value: bfloat16 [1024, 16384], P('tp', 'ctx')
- grad_proj: float32 [1024, 64], P('tp')
- grad_basis: float32 [64, 33], replicated
Inputs may be any that keep to these rules, and one draw needn't show every extreme that they name: decay_rate is positive in every channel.
All inputs are finite; a program needn't handle non-finite values.
Results may differ from a plain program's by a relative error of at most 0.0066.
Values may be sent and summed in bfloat16 or wider, within the bound.
No kernel may reach another device: no remote copies, remote signals or barrier semaphores. Data moves between devices by JAX's collectives and lax.ppermute only.
A program may use at most 64 MiB of HBM per device.

v0:
```python
import math
import jax
import jax.numpy as jnp
from jax import lax
from jax.sharding import PartitionSpec as P

PRECISE = lax.Precision.HIGHEST


def passed_along(value, axis, steps):
    count = lax.axis_size(axis)
    leading, last = (max(0, -steps), min(count, count - steps))
    return lax.ppermute(value, axis, [(source, source + steps) for source in range(leading, last)])


def features(offset_pos, num_pos, seq_total, num_freq):
    positions = offset_pos + jnp.arange(num_pos, dtype=jnp.int32)
    pieces = [positions.astype(jnp.float32) / seq_total]
    for harmonic in range(1, num_freq + 1):
        angles = (harmonic * positions % seq_total).astype(jnp.float32) * (
            2.0 * math.pi / seq_total
        )
        pieces.append(jnp.cos(angles))
        pieces.append(jnp.sin(angles))
    return jnp.stack(pieces)


def window(decay_rate, offset_pos, num_pos, seq_total):
    positions = (offset_pos + jnp.arange(num_pos, dtype=jnp.int32)).astype(jnp.float32)
    energy = jnp.expm1(-2.0 * decay_rate) / jnp.expm1(-2.0 * decay_rate / seq_total)
    return (
        jnp.exp(-(decay_rate[:, None] * positions[None, :]) / seq_total) / jnp.sqrt(energy)[:, None]
    )


def featurize_rim(signal, before, kernel):
    extended = jnp.concatenate([before, signal], axis=1).astype(jnp.float32)
    num_taps = kernel.shape[1]
    rim_len = num_taps - 1
    num_tok = signal.shape[1]
    result = kernel[:, 0:1] * extended[:, rim_len:]
    for offset in range(1, num_taps):
        result = (
            result
            + kernel[:, offset : offset + 1]
            * extended[:, rim_len - offset : rim_len - offset + num_tok]
        )
    return result


def featurize_back(signal, following, kernel):
    extended = jnp.concatenate([signal, following], axis=1).astype(jnp.float32)
    num_taps = kernel.shape[1]
    num_tok = signal.shape[1]
    result = kernel[:, 0:1] * extended[:, :num_tok]
    for offset in range(1, num_taps):
        result = result + kernel[:, offset : offset + 1] * extended[:, offset : offset + num_tok]
    return result


def tables(num_rows, num_cols, modulus):
    row_ids = jnp.arange(num_rows, dtype=jnp.int32)[:, None]
    col_ids = jnp.arange(num_cols, dtype=jnp.int32)[None, :]
    angles = (row_ids * col_ids % modulus).astype(jnp.float32) * (-2.0 * math.pi / modulus)
    return (jnp.cos(angles), jnp.sin(angles))


def spectrum(signal, outer, twiddle, inner):
    num_chan = signal.shape[0]
    folded = signal.reshape(num_chan, outer[0].shape[1], inner[0].shape[0])
    section_re = jnp.einsum("kt,nts->nks", outer[0], folded, precision=PRECISE)
    section_im = jnp.einsum("kt,nts->nks", outer[1], folded, precision=PRECISE)
    turned_re = section_re * twiddle[0] - section_im * twiddle[1]
    turned_im = section_re * twiddle[1] + section_im * twiddle[0]
    spec_re = jnp.einsum("nks,sj->nkj", turned_re, inner[0], precision=PRECISE) - jnp.einsum(
        "nks,sj->nkj", turned_im, inner[1], precision=PRECISE
    )
    spec_im = jnp.einsum("nks,sj->nkj", turned_re, inner[1], precision=PRECISE) + jnp.einsum(
        "nks,sj->nkj", turned_im, inner[0], precision=PRECISE
    )
    return (spec_re, spec_im)


def restore(spec_re, spec_im, outer, twiddle, inner):
    num_chan = spec_re.shape[0]
    padded_len = outer[0].shape[0] * inner[0].shape[0]
    back_re = jnp.einsum("nkj,sj->nks", spec_re, inner[0], precision=PRECISE) + jnp.einsum(
        "nkj,sj->nks", spec_im, inner[1], precision=PRECISE
    )
    back_im = jnp.einsum("nkj,sj->nks", spec_im, inner[0], precision=PRECISE) - jnp.einsum(
        "nkj,sj->nks", spec_re, inner[1], precision=PRECISE
    )
    turned_re = back_re * twiddle[0] + back_im * twiddle[1]
    turned_im = back_im * twiddle[0] - back_re * twiddle[1]
    result = jnp.einsum("kt,nks->nts", outer[0], turned_re, precision=PRECISE) + jnp.einsum(
        "kt,nks->nts", outer[1], turned_im, precision=PRECISE
    )
    return result.reshape(num_chan, -1) * (1.0 / padded_len)


def convolve_forward(carried_chan, filter_chan, own_skip, transform_tables):
    outer, twiddle, inner = transform_tables
    carried_wide = carried_chan.astype(jnp.float32)
    carried_re, carried_im = spectrum(carried_wide, outer, twiddle, inner)
    filter_re, filter_im = spectrum(filter_chan.astype(jnp.float32), outer, twiddle, inner)
    conv_chan = restore(
        filter_re * carried_re - filter_im * carried_im,
        filter_re * carried_im + filter_im * carried_re,
        outer,
        twiddle,
        inner,
    )
    long_chan = (conv_chan + own_skip[:, None] * carried_wide).astype(jnp.bfloat16)
    return (long_chan, (carried_re, carried_im, filter_re, filter_im))


def convolve_backward(grad_chan, spectra, own_skip, transform_tables):
    outer, twiddle, inner = transform_tables
    carried_re, carried_im, filter_re, filter_im = spectra
    grad_chan_wide = grad_chan.astype(jnp.float32)
    grad_re, grad_im = spectrum(grad_chan_wide, outer, twiddle, inner)
    carried_grad_chan = (
        restore(
            filter_re * grad_re + filter_im * grad_im,
            filter_re * grad_im - filter_im * grad_re,
            outer,
            twiddle,
            inner,
        )
        + own_skip[:, None] * grad_chan_wide
    ).astype(jnp.bfloat16)
    filter_grad_chan = restore(
        carried_re * grad_re + carried_im * grad_im,
        carried_re * grad_im - carried_im * grad_re,
        outer,
        twiddle,
        inner,
    ).astype(jnp.bfloat16)
    return (carried_grad_chan, filter_grad_chan)


def on_device(
    query_in,
    key_in,
    value_in,
    short_kernel,
    basis_weight,
    basis_bias,
    filter_proj,
    decay_rate,
    skip_gain,
    grad_out,
):
    ctx_size = lax.axis_size("ctx")
    ctx_rank = lax.axis_index("ctx")
    tp_size = lax.axis_size("tp")
    num_tok = query_in.shape[1]
    chan_local = query_in.shape[0]
    seq_total = num_tok * ctx_size
    all_channels = chan_local * tp_size
    num_freq = (basis_weight.shape[1] - 1) // 2
    feat_width = basis_weight.shape[0]
    rim_len = short_kernel.shape[2] - 1
    tok_start = ctx_rank * num_tok
    rim_edge = num_tok - rim_len
    per_dev = chan_local // ctx_size
    chan_start = ctx_rank * per_dev
    own_skip = lax.dynamic_slice_in_dim(skip_gain, chan_start, per_dev)
    proj_scale = 1.0 / math.sqrt(seq_total)
    basis_scale = math.sqrt(feat_width / (seq_total * all_channels))
    before = passed_along(
        (query_in[:, rim_edge:], key_in[:, rim_edge:], value_in[:, rim_edge:]), "ctx", 1
    )
    query_feat = featurize_rim(query_in, before[0], short_kernel[0])
    key_feat = featurize_rim(key_in, before[1], short_kernel[1])
    value_feat = featurize_rim(value_in, before[2], short_kernel[2])
    carried = (key_feat * value_feat).astype(jnp.bfloat16)
    grad_wide = grad_out.astype(jnp.float32)
    grad_long = (grad_wide * query_feat).astype(jnp.bfloat16)
    basis_rows = features(tok_start, num_tok, seq_total, num_freq)
    hidden_in = (
        jnp.dot(basis_weight, basis_rows, precision=PRECISE, preferred_element_type=jnp.float32)
        + basis_bias[:, None]
    )
    activation = jnp.sin(hidden_in)
    envelope = window(decay_rate, tok_start, num_tok, seq_total)
    filter_tok = (
        jnp.dot(filter_proj, activation, precision=PRECISE, preferred_element_type=jnp.float32)
        * envelope
    ).astype(jnp.bfloat16)
    inner_len = 2 * ctx_size
    transform_tables = (
        tables(num_tok, num_tok // 2, num_tok),
        tables(num_tok, inner_len, 2 * seq_total),
        tables(inner_len, inner_len, inner_len),
    )
    spread = (
        lax.all_to_all(carried, "ctx", split_axis=0, concat_axis=1, tiled=True),
        lax.all_to_all(filter_tok, "ctx", split_axis=0, concat_axis=1, tiled=True),
    )
    carried_chan = spread[0]
    filter_chan = spread[1]
    long_chan, spectra = convolve_forward(carried_chan, filter_chan, own_skip, transform_tables)
    long_tok = lax.all_to_all(long_chan, "ctx", split_axis=1, concat_axis=0, tiled=True)
    grad_chan = lax.all_to_all(grad_long, "ctx", split_axis=0, concat_axis=1, tiled=True)
    carried_grad_chan, filter_grad_chan = convolve_backward(
        grad_chan, spectra, own_skip, transform_tables
    )
    returned = (
        lax.all_to_all(carried_grad_chan, "ctx", split_axis=1, concat_axis=0, tiled=True),
        lax.all_to_all(filter_grad_chan, "ctx", split_axis=1, concat_axis=0, tiled=True),
    )
    carried_grad = returned[0]
    filter_grad_tok = returned[1]
    long_wide = long_tok.astype(jnp.float32)
    mixed = (query_feat * long_wide).astype(jnp.bfloat16)
    grad_query_feat = (grad_wide * long_wide).astype(jnp.bfloat16)
    grad_raw = filter_grad_tok.astype(jnp.float32) * envelope
    part_proj = jnp.dot(
        grad_raw, activation.T, precision=PRECISE, preferred_element_type=jnp.float32
    )
    grad_hidden = jnp.dot(
        filter_proj.T, grad_raw, precision=PRECISE, preferred_element_type=jnp.float32
    ) * jnp.cos(hidden_in)
    part_basis = jnp.dot(
        grad_hidden, basis_rows.T, precision=PRECISE, preferred_element_type=jnp.float32
    )
    grad_proj = lax.psum(part_proj, "ctx") * proj_scale
    grad_basis = lax.psum(part_basis, ("ctx", "tp")) * basis_scale
    carried_grad_wide = carried_grad.astype(jnp.float32)
    grad_key_feat = (carried_grad_wide * value_feat).astype(jnp.bfloat16)
    grad_value_feat = (carried_grad_wide * key_feat).astype(jnp.bfloat16)
    following = passed_along(
        (grad_query_feat[:, :rim_len], grad_key_feat[:, :rim_len], grad_value_feat[:, :rim_len]),
        "ctx",
        -1,
    )
    grad_query = featurize_back(grad_query_feat, following[0], short_kernel[0]).astype(jnp.bfloat16)
    grad_key = featurize_back(grad_key_feat, following[1], short_kernel[1]).astype(jnp.bfloat16)
    grad_value = featurize_back(grad_value_feat, following[2], short_kernel[2]).astype(jnp.bfloat16)
    return (mixed, grad_query, grad_key, grad_value, grad_proj, grad_basis)


def solution(mesh):
    return jax.shard_map(
        on_device,
        mesh=mesh,
        in_specs=(
            P("tp", "ctx"),
            P("tp", "ctx"),
            P("tp", "ctx"),
            P(None, "tp", None),
            P(),
            P(),
            P("tp", None),
            P("tp"),
            P("tp"),
            P("tp", "ctx"),
        ),
        out_specs=(
            P("tp", "ctx"),
            P("tp", "ctx"),
            P("tp", "ctx"),
            P("tp", "ctx"),
            P("tp", None),
            P(),
        ),
        check_vma=False,
    )
```

profile of v0, /device:TPU:1, one launch (start us, length us, event | category | flops | bytes accessed | tf_op | source)
XLA Modules:
  0.0 538.5 jit_solution(8369667688324918726)
XLA Ops:
  0.6 0.8 slice.242
  1.5 4.6 collective-permute-start
  7.5 0.6 copy-done.9
  9.7 0.7 all_to_all.60
  10.4 15.5 %all-to-all-start = ((bf16[64,2,256]{2,1,0:T(2,128)(2,1)}), bf16[64,2,256]{2,1,0:T(2,128)(2,1)S(1)}, u32[]{:S(2)}, u32[]{:S(2)}) async-start(bf16[64,2,256]{2,1,0:T(2,128)(2,1)} %all_to_all.60), calls=%async_computation | async-start | bytes 131072 | tf_op jit(solution)/shard_map/all_to_all | solution.py:199
  26.0 3.5 collective-permute-start.2
  29.6 2.2 collective-permute-start.1
  33.1 0.6 copy-done.8
  33.9 0.7 copy-done.1
  35.1 0.7 all_to_all.67
  35.7 2.4 all-to-all-done
  38.1 9.7 %all-to-all-start.3 = ((bf16[64,2,256]{2,1,0:T(2,128)(2,1)}), bf16[64,2,256]{2,1,0:T(2,128)(2,1)S(1)}, u32[]{:S(2)}, u32[]{:S(2)}) async-start(bf16[64,2,256]{2,1,0:T(2,128)(2,1)} %all_to_all.67), calls=%async_computation.3 | async-start | bytes 131072 | tf_op jit(solution)/shard_map/all_to_all | solution.py:205
  47.8 0.8 convolution_bitcast_fusion.4
  48.6 0.8 convolution_bitcast_fusion.5
  49.4 0.8 fusion.144
  50.1 0.8 convolution_subtract_fusion.5
  50.9 0.8 fusion.121
  51.7 7.9 %all-to-all-done.3 = bf16[64,2,256]{2,1,0:T(2,128)(2,1)S(1)} async-done(((bf16[64,2,256]{2,1,0:T(2,128)(2,1)}), bf16[64,2,256]{2,1,0:T(2,128)(2,1)S(1)}, u32[]{:S(2)}, u32[]{:S(2)}) %all-to-all-start.3) | async-done | bytes 65568 | tf_op jit(solution)/shard_map/all_to_all | solution.py:205
  59.6 0.8 convolution_bitcast_fusion
  60.4 0.8 convolution_bitcast_fusion.1
  61.2 0.8 fusion.134
  62.0 0.8 fusion.114
  62.7 0.8 convolution_subtract_fusion.2
  63.5 0.8 convolution_add_fusion.2
  64.3 0.8 multiply_add_fusion.1
  66.3 0.6 convolution_add_fusion.1
  66.9 0.6 convolution_subtract_fusion.1
  67.6 11.5 %fusion.19 = f32[2,128,128]{2,1,0:T(8,128)S(1)} fusion(f32[2,256,128]{1,2,0:T(8,128)S(1)} %convolution_subtract_fusion.1, f32[2,256,128]{1,2,0:T(8,128)S(1)} %convolution_add_fusion.1, f32[256,128]{0,1:T(8,128)S(1)} %copy.206, f32[256,128]{0,1:T(8,128)S(1)} %copy.204), kind=kOutput, calls=%fused_computation.45 | convolution fusion | flops 101318656 | bytes 917504 | tf_op jit(solution)/shard_map/kt,nks->nts/dot_general | solution.py:95
  79.1 0.9 fusion.2
  80.2 0.7 copy.236
  80.9 4.8 all-to-all-start.4
  86.0 12.0 %all-to-all-done.4 = bf16[2,64,256]{2,0,1:T(2,128)(2,1)S(1)} async-done(((bf16[2,64,256]{2,0,1:T(2,128)(2,1)}), bf16[2,64,256]{2,0,1:T(2,128)(2,1)S(1)}, u32[]{:S(2)}, u32[]{:S(2)}) %all-to-all-start.4) | async-done | bytes 65568 | tf_op jit(solution)/shard_map/all_to_all | solution.py:210
  98.5 2.3 collective-permute-start.5
  101.3 0.7 all_to_all.63
  101.9 6.0 %all-to-all-start.1 = ((bf16[64,2,256]{2,1,0:T(2,128)(2,1)}), bf16[64,2,256]{2,1,0:T(2,128)(2,1)S(1)}, u32[]{:S(2)}, u32[]{:S(2)}) async-start(bf16[64,2,256]{2,1,0:T(2,128)(2,1)} %all_to_all.63), calls=%async_computation.1 | async-start | bytes 131072 | tf_op jit(solution)/shard_map/all_to_all | solution.py:198
  108.0 2.4 collective-permute-start.4
  110.4 1.0 fusion.37
  111.4 2.1 collective-permute-done.4
  113.5 1.0 fusion.44
  114.5 5.6 %all-to-all-done.1 = bf16[64,2,256]{2,1,0:T(2,128)(2,1)S(1)} async-done(((bf16[64,2,256]{2,1,0:T(2,128)(2,1)}), bf16[64,2,256]{2,1,0:T(2,128)(2,1)S(1)}, u32[]{:S(2)}, u32[]{:S(2)}) %all-to-all-start.1) | async-done | bytes 65568 | tf_op jit(solution)/shard_map/all_to_all | solution.py:198
  120.2 0.8 convolution_bitcast_fusion.2
  121.0 0.8 convolution_bitcast_fusion.3
  121.8 0.8 fusion.119
  122.5 0.8 fusion.142
  123.3 0.8 convolution_subtract_fusion.4
  124.0 0.8 multiply_add_fusion
  126.1 0.6 convolution_add_fusion
  126.8 0.6 convolution_subtract_fusion
  127.4 0.9 fusion.12
  128.3 0.9 fusion.8
  129.3 0.7 copy.242
  130.0 7.0 %all-to-all-start.5 = ((bf16[2,64,256]{2,0,1:T(2,128)(2,1)}), bf16[2,64,256]{2,0,1:T(2,128)(2,1)S(1)}, u32[]{:S(2)}, u32[]{:S(2)}) async-start(bf16[2,64,256]{2,0,1:T(2,128)(2,1)} %copy.242), calls=%async_computation.5 | async-start | bytes 131072 | tf_op jit(solution)/shard_map/all_to_all | solution.py:211
  138.3 0.6 convolution_add_fusion.3
  138.9 0.6 convolution_subtract_fusion.3
  139.6 0.9 fusion.26
  140.5 0.9 fusion.4
  141.6 0.7 copy.223
  142.3 6.9 %all-to-all-done.5 = bf16[2,64,256]{2,0,1:T(2,128)(2,1)S(1)} async-done(((bf16[2,64,256]{2,0,1:T(2,128)(2,1)}), bf16[2,64,256]{2,0,1:T(2,128)(2,1)S(1)}, u32[]{:S(2)}, u32[]{:S(2)}) %all-to-all-start.5) | async-done | bytes 65568 | tf_op jit(solution)/shard_map/all_to_all | solution.py:211
  149.2 5.8 %all-to-all-start.2 = ((bf16[2,64,256]{2,0,1:T(2,128)(2,1)}), bf16[2,64,256]{2,0,1:T(2,128)(2,1)S(1)}, u32[]{:S(2)}, u32[]{:S(2)}) async-start(bf16[2,64,256]{2,0,1:T(2,128)(2,1)} %copy.223), calls=%async_computation.2 | async-start | bytes 131072 | tf_op jit(solution)/shard_map/all_to_all | solution.py:204
  156.2 99.6 %psum.15 = f32[64,33]{0,1:T(8,128)S(1)} all-reduce(f32[64,33]{0,1:T(8,128)S(1)} %fusion.423), channel_id=1, replica_groups=mesh['ctx'=64,'tp'=8] {'ctx','tp'}, use_global_device_ids=true, to_apply=%region_1.2 | all-reduce | flops 2112 | bytes 16896 | tf_op jit(solution)/shard_map/psum | solution.py:229
  255.8 270.7 %psum.14 = f32[128,64]{0,1:T(8,128)S(1)} all-reduce(f32[128,64]{0,1:T(8,128)S(1)} %fusion.417), channel_id=1, replica_groups=mesh['ctx'=64,'tp'=8] {'ctx'}, use_global_device_ids=true, to_apply=%region_0.1 | all-reduce | flops 8192 | bytes 65536 | tf_op jit(solution)/shard_map/psum | solution.py:228
  527.3 0.7 fusion.30
  528.0 8.4 %collective-permute-start.3 = (bf16[128,6]{1,0:T(8,128)(2,1)S(1)}, bf16[128,6]{1,0:T(8,128)(2,1)S(1)}, u32[]{:S(2)}, u32[]{:S(2)}) collective-permute-start(bf16[128,6]{1,0:T(8,128)(2,1)S(1)} %slice.333), channel_id=1, source_target_pairs={{8,0},{16,8},{24,16},{32,24},{40,32},{48,40},{56,48},{64,56},{72,6... | collective-permute-start | bytes 4616 | tf_op jit(solution)/shard_map/ppermute | solution.py:13
  537.3 1.0 fusion.51
  (100 shorter events, 13.3 us)
Async XLA Ops:
  0.6 8.8 %copy-start = (f32[128,64]{0,1:T(8,128)S(1)}, f32[128,64]{0,1:T(8,128)}, u32[]{:S(2)}) copy-start(f32[128,64]{0,1:T(8,128)} %param.16) | copy-start | bytes 98308
  1.5 32.3 %collective-permute-start = (bf16[128,6]{1,0:T(8,128)(2,1)S(1)}, bf16[128,6]{1,0:T(8,128)(2,1)S(1)}, u32[]{:S(2)}, u32[]{:S(2)}) collective-permute-start(bf16[128,6]{1,0:T(8,128)(2,1)S(1)} %slice.242), channel_id=1, source_target_pairs={{0,8},{8,16},{16,24},{24,32},{32,40},{40,48},{48,56},{56,64},{64,7... | collective-permute-start | bytes 4616 | tf_op jit(solution)/shard_map/ppermute | solution.py:13
  7.5 0.7 copy-start.9
  8.2 0.7 copy-start.5
  8.2 0.7 copy-start.7
  10.4 15.5 %copy-start.3 = (bf16[128,256]{1,0:T(8,128)(2,1)S(1)}, bf16[128,256]{1,0:T(8,128)(2,1)}, u32[]{:S(2)}) copy-start(bf16[128,256]{1,0:T(8,128)(2,1)} %param.12) | copy-start | bytes 196612
  10.4 27.7 %all-to-all-start = ((bf16[64,2,256]{2,1,0:T(2,128)(2,1)}), bf16[64,2,256]{2,1,0:T(2,128)(2,1)S(1)}, u32[]{:S(2)}, u32[]{:S(2)}) async-start(bf16[64,2,256]{2,1,0:T(2,128)(2,1)} %all_to_all.60), calls=%async_computation | async-start | bytes 131072 | tf_op jit(solution)/shard_map/all_to_all | solution.py:199
  25.9 3.6 copy-start.4
  26.0 59.8 %collective-permute-start.2 = (bf16[128,6]{1,0:T(8,128)(2,1)S(1)}, bf16[128,6]{1,0:T(8,128)(2,1)S(1)}, u32[]{:S(2)}, u32[]{:S(2)}) collective-permute-start(bf16[128,6]{1,0:T(8,128)(2,1)S(1)} %slice.274), channel_id=1, source_target_pairs={{0,8},{8,16},{16,24},{24,32},{32,40},{40,48},{48,56},{56,64},{64,7... | collective-permute-start | bytes 4616 | tf_op jit(solution)/shard_map/ppermute | solution.py:13
  29.6 2.7 copy-start.6
  29.6 56.3 %collective-permute-start.1 = (bf16[128,6]{1,0:T(8,128)(2,1)S(1)}, bf16[128,6]{1,0:T(8,128)(2,1)S(1)}, u32[]{:S(2)}, u32[]{:S(2)}) collective-permute-start(bf16[128,6]{1,0:T(8,128)(2,1)S(1)} %slice.258), channel_id=1, source_target_pairs={{0,8},{8,16},{16,24},{24,32},{32,40},{40,48},{48,56},{56,64},{64,7... | collective-permute-start | bytes 4616 | tf_op jit(solution)/shard_map/ppermute | solution.py:13
  33.0 0.9 copy-start.2
  33.1 0.7 copy-start.8
  33.8 0.8 copy-start.1
  38.1 21.5 %all-to-all-start.3 = ((bf16[64,2,256]{2,1,0:T(2,128)(2,1)}), bf16[64,2,256]{2,1,0:T(2,128)(2,1)S(1)}, u32[]{:S(2)}, u32[]{:S(2)}) async-start(bf16[64,2,256]{2,1,0:T(2,128)(2,1)} %all_to_all.67), calls=%async_computation.3 | async-start | bytes 131072 | tf_op jit(solution)/shard_map/all_to_all | solution.py:205
  80.9 17.0 %all-to-all-start.4 = ((bf16[2,64,256]{2,0,1:T(2,128)(2,1)}), bf16[2,64,256]{2,0,1:T(2,128)(2,1)S(1)}, u32[]{:S(2)}, u32[]{:S(2)}) async-start(bf16[2,64,256]{2,0,1:T(2,128)(2,1)} %copy.236), calls=%async_computation.4 | async-start | bytes 131072 | tf_op jit(solution)/shard_map/all_to_all | solution.py:210
  98.5 11.8 %collective-permute-start.5 = (bf16[128,6]{1,0:T(8,128)(2,1)S(1)}, bf16[128,6]{1,0:T(8,128)(2,1)S(1)}, u32[]{:S(2)}, u32[]{:S(2)}) collective-permute-start(bf16[128,6]{1,0:T(8,128)(2,1)S(1)} %slice.349), channel_id=1, source_target_pairs={{8,0},{16,8},{24,16},{32,24},{40,32},{48,40},{56,48},{64,56},{72,6... | collective-permute-start | bytes 4616 | tf_op jit(solution)/shard_map/ppermute | solution.py:13
  101.9 18.2 %all-to-all-start.1 = ((bf16[64,2,256]{2,1,0:T(2,128)(2,1)}), bf16[64,2,256]{2,1,0:T(2,128)(2,1)S(1)}, u32[]{:S(2)}, u32[]{:S(2)}) async-start(bf16[64,2,256]{2,1,0:T(2,128)(2,1)} %all_to_all.63), calls=%async_computation.1 | async-start | bytes 131072 | tf_op jit(solution)/shard_map/all_to_all | solution.py:198
  108.0 5.5 %collective-permute-start.4 = (bf16[128,6]{1,0:T(8,128)(2,1)S(1)}, bf16[128,6]{1,0:T(8,128)(2,1)S(1)}, u32[]{:S(2)}, u32[]{:S(2)}) collective-permute-start(bf16[128,6]{1,0:T(8,128)(2,1)S(1)} %slice.341), channel_id=1, source_target_pairs={{8,0},{16,8},{24,16},{32,24},{40,32},{48,40},{56,48},{64,56},{72,6... | collective-permute-start | bytes 4616 | tf_op jit(solution)/shard_map/ppermute | solution.py:13
  130.0 19.1 %all-to-all-start.5 = ((bf16[2,64,256]{2,0,1:T(2,128)(2,1)}), bf16[2,64,256]{2,0,1:T(2,128)(2,1)S(1)}, u32[]{:S(2)}, u32[]{:S(2)}) async-start(bf16[2,64,256]{2,0,1:T(2,128)(2,1)} %copy.242), calls=%async_computation.5 | async-start | bytes 131072 | tf_op jit(solution)/shard_map/all_to_all | solution.py:211
  149.2 378.0 %all-to-all-start.2 = ((bf16[2,64,256]{2,0,1:T(2,128)(2,1)}), bf16[2,64,256]{2,0,1:T(2,128)(2,1)S(1)}, u32[]{:S(2)}, u32[]{:S(2)}) async-start(bf16[2,64,256]{2,0,1:T(2,128)(2,1)} %copy.223), calls=%async_computation.2 | async-start | bytes 131072 | tf_op jit(solution)/shard_map/all_to_all | solution.py:204
  528.0 9.3 %collective-permute-start.3 = (bf16[128,6]{1,0:T(8,128)(2,1)S(1)}, bf16[128,6]{1,0:T(8,128)(2,1)S(1)}, u32[]{:S(2)}, u32[]{:S(2)}) collective-permute-start(bf16[128,6]{1,0:T(8,128)(2,1)S(1)} %slice.333), channel_id=1, source_target_pairs={{8,0},{16,8},{24,16},{32,24},{40,32},{48,40},{56,48},{64,56},{72,6... | collective-permute-start | bytes 4616 | tf_op jit(solution)/shard_map/ppermute | solution.py:13
where the time goes:
time: 544 us; the launch traced here: 539 us
  blocking collectives  370 us (68%)
  starting transfers between devices  72.2 us (13%)
  matrix products  39.1 us (7%)
  waiting for transfers between devices  37.1 us (7%)
  other arithmetic  9.16 us (2%)
  local copies, waits for them, and re-layouts  8.96 us (2%)
    psum x1, blocking collectives, on_device(): grad_proj = lax.psum(part_proj, 'ctx') * proj_scale  271 us
    psum x1, blocking collectives, on_device(): grad_basis = lax.psum(part_basis, ('ctx', 'tp')) * basis_scale  99.6 us
    ppermute x6, starting transfers between devices, passed_along(): lax.ppermute(value, axis, [(source, source + steps) for source in range(l...  23.4 us
    all_to_all x1, starting transfers between devices, on_device(): lax.all_to_all(filter_tok, 'ctx', split_axis=0, concat_axis=1, tiled=True)  15.5 us
    dot_general x3, matrix products, restore(): jnp.einsum('kt,nks->nts', outer[0], turned_re, precision=PRECISE)  13.3 us
    all_to_all x1, waiting for transfers between devices, on_device(): lax.all_to_all(carried_grad_chan, 'ctx', split_axis=1, concat_axis=0, til...  12 us
  transfers between devices with their start and end apart: 12, of which 7 were waited for; matrix products, arithmetic and copies ran while one was open for 7% of the time, Pallas kernels for 0%

commit v1 on v0

--- a/solution.py
+++ b/solution.py
@@ -226,7 +226,7 @@
         grad_hidden, basis_rows.T, precision=PRECISE, preferred_element_type=jnp.float32
     )
     grad_proj = lax.psum(part_proj, "ctx") * proj_scale
-    grad_basis = lax.psum(part_basis, ("ctx", "tp")) * basis_scale
+    grad_basis = lax.psum(lax.psum(part_basis, "tp"), "ctx") * basis_scale
     carried_grad_wide = carried_grad.astype(jnp.float32)
     grad_key_feat = (carried_grad_wide * value_feat).astype(jnp.bfloat16)
     grad_value_feat = (carried_grad_wide * key_feat).astype(jnp.bfloat16)

time: 544 us -> 478 us (0.88)
  blocking collectives: 370 us -> 303 us
    psum x1, blocking collectives: 99.6 us -> 27.7 us  [on_device(): grad_basis = lax.psum(lax.psum(part_basis, 'tp'), 'ctx') * basis_scale]
  transfers between devices with their start and end apart: 12 -> 12, of which waited for: 7 -> 7; matrix products, arithmetic and copies ran while one was open for 7% -> 8% of each run, Pallas kernels for 0% -> 0%
where the time goes in v1:
time: 478 us; the launch traced here: 472 us
  blocking collectives  303 us (63%)
  starting transfers between devices  72.2 us (15%)
  matrix products  39.1 us (8%)
  waiting for transfers between devices  37.1 us (8%)
  other arithmetic  9.16 us (2%)
  local copies, waits for them, and re-layouts  8.96 us (2%)
    psum x1, blocking collectives, on_device(): grad_proj = lax.psum(part_proj, 'ctx') * proj_scale  276 us
    psum x1, blocking collectives, on_device(): grad_basis = lax.psum(lax.psum(part_basis, 'tp'), 'ctx') * basis_scale  27.7 us
    ppermute x6, starting transfers between devices, passed_along(): lax.ppermute(value, axis, [(source, source + steps) for source in range(l...  23.4 us
    all_to_all x1, starting transfers between devices, on_device(): lax.all_to_all(filter_tok, 'ctx', split_axis=0, concat_axis=1, tiled=True)  15.5 us
    dot_general x3, matrix products, restore(): jnp.einsum('kt,nks->nts', outer[0], turned_re, precision=PRECISE)  13.3 us
    all_to_all x1, waiting for transfers between devices, on_device(): lax.all_to_all(carried_grad_chan, 'ctx', split_axis=1, concat_axis=0, til...  12 us
    all_to_all x1, starting transfers between devices, on_device(): lax.all_to_all(grad_long, 'ctx', split_axis=0, concat_axis=1, tiled=True)  9.67 us
  transfers between devices with their start and end apart: 12, of which 7 were waited for; matrix products, arithmetic and copies ran while one was open for 8% of the time, Pallas kernels for 0%

profile of v1, /device:TPU:1, one launch (start us, length us, event | category | flops | bytes accessed | tf_op | source)
XLA Modules:
  0.0 471.6 jit_solution(10600531233884873021)
XLA Ops:
  0.6 0.8 slice.242
  1.5 4.6 collective-permute-start
  7.5 0.6 copy-done.9
  9.7 0.7 all_to_all.60
  10.4 15.5 %all-to-all-start = ((bf16[64,2,256]{2,1,0:T(2,128)(2,1)}), bf16[64,2,256]{2,1,0:T(2,128)(2,1)S(1)}, u32[]{:S(2)}, u32[]{:S(2)}) async-start(bf16[64,2,256]{2,1,0:T(2,128)(2,1)} %all_to_all.60), calls=%async_computation | async-start | bytes 131072 | tf_op jit(solution)/shard_map/all_to_all | solution.py:199
  26.0 3.5 collective-permute-start.2
  29.6 2.2 collective-permute-start.1
  33.1 0.6 copy-done.8
  33.9 0.7 copy-done.1
  35.1 0.7 all_to_all.67
  35.7 2.4 all-to-all-done
  38.1 9.7 %all-to-all-start.3 = ((bf16[64,2,256]{2,1,0:T(2,128)(2,1)}), bf16[64,2,256]{2,1,0:T(2,128)(2,1)S(1)}, u32[]{:S(2)}, u32[]{:S(2)}) async-start(bf16[64,2,256]{2,1,0:T(2,128)(2,1)} %all_to_all.67), calls=%async_computation.3 | async-start | bytes 131072 | tf_op jit(solution)/shard_map/all_to_all | solution.py:205
  47.8 0.8 convolution_bitcast_fusion.4
  48.6 0.8 convolution_bitcast_fusion.5
  49.4 0.8 fusion.144
  50.1 0.8 convolution_subtract_fusion.5
  50.9 0.8 fusion.121
  51.7 7.9 %all-to-all-done.3 = bf16[64,2,256]{2,1,0:T(2,128)(2,1)S(1)} async-done(((bf16[64,2,256]{2,1,0:T(2,128)(2,1)}), bf16[64,2,256]{2,1,0:T(2,128)(2,1)S(1)}, u32[]{:S(2)}, u32[]{:S(2)}) %all-to-all-start.3) | async-done | bytes 65568 | tf_op jit(solution)/shard_map/all_to_all | solution.py:205
  59.6 0.8 convolution_bitcast_fusion
  60.4 0.8 convolution_bitcast_fusion.1
  61.2 0.8 fusion.134
  62.0 0.8 fusion.114
  62.7 0.8 convolution_subtract_fusion.2
  63.5 0.8 convolution_add_fusion.2
  64.3 0.8 multiply_add_fusion.1
  66.3 0.6 convolution_add_fusion.1
  66.9 0.6 convolution_subtract_fusion.1
  67.6 11.5 %fusion.19 = f32[2,128,128]{2,1,0:T(8,128)S(1)} fusion(f32[2,256,128]{1,2,0:T(8,128)S(1)} %convolution_subtract_fusion.1, f32[2,256,128]{1,2,0:T(8,128)S(1)} %convolution_add_fusion.1, f32[256,128]{0,1:T(8,128)S(1)} %copy.206, f32[256,128]{0,1:T(8,128)S(1)} %copy.204), kind=kOutput, calls=%fused_computation.45 | convolution fusion | flops 101318656 | bytes 917504 | tf_op jit(solution)/shard_map/kt,nks->nts/dot_general | solution.py:95
  79.1 0.9 fusion.2
  80.2 0.7 copy.236
  80.9 4.8 %all-to-all-start.4 = ((bf16[2,64,256]{2,0,1:T(2,128)(2,1)}), bf16[2,64,256]{2,0,1:T(2,128)(2,1)S(1)}, u32[]{:S(2)}, u32[]{:S(2)}) async-start(bf16[2,64,256]{2,0,1:T(2,128)(2,1)} %copy.236), calls=%async_computation.4 | async-start | bytes 131072 | tf_op jit(solution)/shard_map/all_to_all | solution.py:210
  86.0 12.0 %all-to-all-done.4 = bf16[2,64,256]{2,0,1:T(2,128)(2,1)S(1)} async-done(((bf16[2,64,256]{2,0,1:T(2,128)(2,1)}), bf16[2,64,256]{2,0,1:T(2,128)(2,1)S(1)}, u32[]{:S(2)}, u32[]{:S(2)}) %all-to-all-start.4) | async-done | bytes 65568 | tf_op jit(solution)/shard_map/all_to_all | solution.py:210
  98.5 2.3 collective-permute-start.5
  101.3 0.7 all_to_all.63
  101.9 6.0 %all-to-all-start.1 = ((bf16[64,2,256]{2,1,0:T(2,128)(2,1)}), bf16[64,2,256]{2,1,0:T(2,128)(2,1)S(1)}, u32[]{:S(2)}, u32[]{:S(2)}) async-start(bf16[64,2,256]{2,1,0:T(2,128)(2,1)} %all_to_all.63), calls=%async_computation.1 | async-start | bytes 131072 | tf_op jit(solution)/shard_map/all_to_all | solution.py:198
  108.0 2.4 collective-permute-start.4
  110.4 1.0 fusion.37
  111.4 2.1 collective-permute-done.4
  113.5 1.0 fusion.44
  114.5 5.6 %all-to-all-done.1 = bf16[64,2,256]{2,1,0:T(2,128)(2,1)S(1)} async-done(((bf16[64,2,256]{2,1,0:T(2,128)(2,1)}), bf16[64,2,256]{2,1,0:T(2,128)(2,1)S(1)}, u32[]{:S(2)}, u32[]{:S(2)}) %all-to-all-start.1) | async-done | bytes 65568 | tf_op jit(solution)/shard_map/all_to_all | solution.py:198
  120.2 0.8 convolution_bitcast_fusion.2
  121.0 0.8 convolution_bitcast_fusion.3
  121.8 0.8 fusion.119
  122.5 0.8 fusion.142
  123.3 0.8 convolution_subtract_fusion.4
  124.0 0.8 multiply_add_fusion
  126.1 0.6 convolution_add_fusion
  126.8 0.6 convolution_subtract_fusion
  127.4 0.9 fusion.12
  128.3 0.9 fusion.8
  129.3 0.7 copy.242
  130.0 7.0 %all-to-all-start.5 = ((bf16[2,64,256]{2,0,1:T(2,128)(2,1)}), bf16[2,64,256]{2,0,1:T(2,128)(2,1)S(1)}, u32[]{:S(2)}, u32[]{:S(2)}) async-start(bf16[2,64,256]{2,0,1:T(2,128)(2,1)} %copy.242), calls=%async_computation.5 | async-start | bytes 131072 | tf_op jit(solution)/shard_map/all_to_all | solution.py:211
  138.3 0.6 convolution_add_fusion.3
  138.9 0.6 convolution_subtract_fusion.3
  139.6 0.9 fusion.26
  140.5 0.9 fusion.4
  141.6 0.7 copy.223
  142.3 6.9 %all-to-all-done.5 = bf16[2,64,256]{2,0,1:T(2,128)(2,1)S(1)} async-done(((bf16[2,64,256]{2,0,1:T(2,128)(2,1)}), bf16[2,64,256]{2,0,1:T(2,128)(2,1)S(1)}, u32[]{:S(2)}, u32[]{:S(2)}) %all-to-all-start.5) | async-done | bytes 65568 | tf_op jit(solution)/shard_map/all_to_all | solution.py:211
  149.2 5.8 %all-to-all-start.2 = ((bf16[2,64,256]{2,0,1:T(2,128)(2,1)}), bf16[2,64,256]{2,0,1:T(2,128)(2,1)S(1)}, u32[]{:S(2)}, u32[]{:S(2)}) async-start(bf16[2,64,256]{2,0,1:T(2,128)(2,1)} %copy.223), calls=%async_computation.2 | async-start | bytes 131072 | tf_op jit(solution)/shard_map/all_to_all | solution.py:204
  156.2 27.7 %psum.22 = f32[64,33]{0,1:T(8,128)S(1)} all-reduce(f32[64,33]{0,1:T(8,128)S(1)} %fusion.423), channel_id=1, replica_groups=mesh['ctx'=64,'tp'=8] {'tp'}, use_global_device_ids=true, to_apply=%region_1.2 | all-reduce | flops 2112 | bytes 16896 | tf_op jit(solution)/shard_map/psum | solution.py:229
  183.9 275.7 %all-reduce = (f32[128,64]{0,1:T(8,128)S(1)}, f32[64,33]{0,1:T(8,128)S(1)}) all-reduce(f32[128,64]{0,1:T(8,128)S(1)} %fusion.417, f32[64,33]{0,1:T(8,128)S(1)} %psum.22), channel_id=1, replica_groups=mesh['ctx'=64,'tp'=8] {'ctx'}, use_global_device_ids=true, to_apply=%region_0.1 | all-reduce | flops 10304 | bytes 82432 | tf_op jit(solution)/shard_map/psum | solution.py:228
  460.4 0.7 fusion.30
  461.0 8.4 %collective-permute-start.3 = (bf16[128,6]{1,0:T(8,128)(2,1)S(1)}, bf16[128,6]{1,0:T(8,128)(2,1)S(1)}, u32[]{:S(2)}, u32[]{:S(2)}) collective-permute-start(bf16[128,6]{1,0:T(8,128)(2,1)S(1)} %slice.333), channel_id=1, source_target_pairs={{8,0},{16,8},{24,16},{32,24},{40,32},{48,40},{56,48},{64,56},{72,6... | collective-permute-start | bytes 4616 | tf_op jit(solution)/shard_map/ppermute | solution.py:13
  470.4 1.0 fusion.51
  (100 shorter events, 13.3 us)
Async XLA Ops:
  0.6 8.8 %copy-start = (f32[128,64]{0,1:T(8,128)S(1)}, f32[128,64]{0,1:T(8,128)}, u32[]{:S(2)}) copy-start(f32[128,64]{0,1:T(8,128)} %param.16) | copy-start | bytes 98308
  1.5 32.3 %collective-permute-start = (bf16[128,6]{1,0:T(8,128)(2,1)S(1)}, bf16[128,6]{1,0:T(8,128)(2,1)S(1)}, u32[]{:S(2)}, u32[]{:S(2)}) collective-permute-start(bf16[128,6]{1,0:T(8,128)(2,1)S(1)} %slice.242), channel_id=1, source_target_pairs={{0,8},{8,16},{16,24},{24,32},{32,40},{40,48},{48,56},{56,64},{64,7... | collective-permute-start | bytes 4616 | tf_op jit(solution)/shard_map/ppermute | solution.py:13
  7.5 0.7 copy-start.9
  8.2 0.7 copy-start.5
  8.2 0.7 copy-start.7
  10.4 15.5 %copy-start.3 = (bf16[128,256]{1,0:T(8,128)(2,1)S(1)}, bf16[128,256]{1,0:T(8,128)(2,1)}, u32[]{:S(2)}) copy-start(bf16[128,256]{1,0:T(8,128)(2,1)} %param.12) | copy-start | bytes 196612
  10.4 27.7 %all-to-all-start = ((bf16[64,2,256]{2,1,0:T(2,128)(2,1)}), bf16[64,2,256]{2,1,0:T(2,128)(2,1)S(1)}, u32[]{:S(2)}, u32[]{:S(2)}) async-start(bf16[64,2,256]{2,1,0:T(2,128)(2,1)} %all_to_all.60), calls=%async_computation | async-start | bytes 131072 | tf_op jit(solution)/shard_map/all_to_all | solution.py:199
  25.9 3.6 copy-start.4
  26.0 59.8 %collective-permute-start.2 = (bf16[128,6]{1,0:T(8,128)(2,1)S(1)}, bf16[128,6]{1,0:T(8,128)(2,1)S(1)}, u32[]{:S(2)}, u32[]{:S(2)}) collective-permute-start(bf16[128,6]{1,0:T(8,128)(2,1)S(1)} %slice.274), channel_id=1, source_target_pairs={{0,8},{8,16},{16,24},{24,32},{32,40},{40,48},{48,56},{56,64},{64,7... | collective-permute-start | bytes 4616 | tf_op jit(solution)/shard_map/ppermute | solution.py:13
  29.6 2.7 copy-start.6
  29.6 56.3 %collective-permute-start.1 = (bf16[128,6]{1,0:T(8,128)(2,1)S(1)}, bf16[128,6]{1,0:T(8,128)(2,1)S(1)}, u32[]{:S(2)}, u32[]{:S(2)}) collective-permute-start(bf16[128,6]{1,0:T(8,128)(2,1)S(1)} %slice.258), channel_id=1, source_target_pairs={{0,8},{8,16},{16,24},{24,32},{32,40},{40,48},{48,56},{56,64},{64,7... | collective-permute-start | bytes 4616 | tf_op jit(solution)/shard_map/ppermute | solution.py:13
  33.0 0.9 copy-start.2
  33.1 0.7 copy-start.8
  33.8 0.8 copy-start.1
  38.1 21.5 %all-to-all-start.3 = ((bf16[64,2,256]{2,1,0:T(2,128)(2,1)}), bf16[64,2,256]{2,1,0:T(2,128)(2,1)S(1)}, u32[]{:S(2)}, u32[]{:S(2)}) async-start(bf16[64,2,256]{2,1,0:T(2,128)(2,1)} %all_to_all.67), calls=%async_computation.3 | async-start | bytes 131072 | tf_op jit(solution)/shard_map/all_to_all | solution.py:205
  80.9 17.0 %all-to-all-start.4 = ((bf16[2,64,256]{2,0,1:T(2,128)(2,1)}), bf16[2,64,256]{2,0,1:T(2,128)(2,1)S(1)}, u32[]{:S(2)}, u32[]{:S(2)}) async-start(bf16[2,64,256]{2,0,1:T(2,128)(2,1)} %copy.236), calls=%async_computation.4 | async-start | bytes 131072 | tf_op jit(solution)/shard_map/all_to_all | solution.py:210
  98.5 11.8 %collective-permute-start.5 = (bf16[128,6]{1,0:T(8,128)(2,1)S(1)}, bf16[128,6]{1,0:T(8,128)(2,1)S(1)}, u32[]{:S(2)}, u32[]{:S(2)}) collective-permute-start(bf16[128,6]{1,0:T(8,128)(2,1)S(1)} %slice.349), channel_id=1, source_target_pairs={{8,0},{16,8},{24,16},{32,24},{40,32},{48,40},{56,48},{64,56},{72,6... | collective-permute-start | bytes 4616 | tf_op jit(solution)/shard_map/ppermute | solution.py:13
  101.9 18.2 %all-to-all-start.1 = ((bf16[64,2,256]{2,1,0:T(2,128)(2,1)}), bf16[64,2,256]{2,1,0:T(2,128)(2,1)S(1)}, u32[]{:S(2)}, u32[]{:S(2)}) async-start(bf16[64,2,256]{2,1,0:T(2,128)(2,1)} %all_to_all.63), calls=%async_computation.1 | async-start | bytes 131072 | tf_op jit(solution)/shard_map/all_to_all | solution.py:198
  108.0 5.5 %collective-permute-start.4 = (bf16[128,6]{1,0:T(8,128)(2,1)S(1)}, bf16[128,6]{1,0:T(8,128)(2,1)S(1)}, u32[]{:S(2)}, u32[]{:S(2)}) collective-permute-start(bf16[128,6]{1,0:T(8,128)(2,1)S(1)} %slice.341), channel_id=1, source_target_pairs={{8,0},{16,8},{24,16},{32,24},{40,32},{48,40},{56,48},{64,56},{72,6... | collective-permute-start | bytes 4616 | tf_op jit(solution)/shard_map/ppermute | solution.py:13
  130.0 19.1 %all-to-all-start.5 = ((bf16[2,64,256]{2,0,1:T(2,128)(2,1)}), bf16[2,64,256]{2,0,1:T(2,128)(2,1)S(1)}, u32[]{:S(2)}, u32[]{:S(2)}) async-start(bf16[2,64,256]{2,0,1:T(2,128)(2,1)} %copy.242), calls=%async_computation.5 | async-start | bytes 131072 | tf_op jit(solution)/shard_map/all_to_all | solution.py:211
  149.2 311.1 %all-to-all-start.2 = ((bf16[2,64,256]{2,0,1:T(2,128)(2,1)}), bf16[2,64,256]{2,0,1:T(2,128)(2,1)S(1)}, u32[]{:S(2)}, u32[]{:S(2)}) async-start(bf16[2,64,256]{2,0,1:T(2,128)(2,1)} %copy.223), calls=%async_computation.2 | async-start | bytes 131072 | tf_op jit(solution)/shard_map/all_to_all | solution.py:204
  461.0 9.3 %collective-permute-start.3 = (bf16[128,6]{1,0:T(8,128)(2,1)S(1)}, bf16[128,6]{1,0:T(8,128)(2,1)S(1)}, u32[]{:S(2)}, u32[]{:S(2)}) collective-permute-start(bf16[128,6]{1,0:T(8,128)(2,1)S(1)} %slice.333), channel_id=1, source_target_pairs={{8,0},{16,8},{24,16},{32,24},{40,32},{48,40},{56,48},{64,56},{72,6... | collective-permute-start | bytes 4616 | tf_op jit(solution)/shard_map/ppermute | solution.py:13
